TPU v7x, 512 devices: a whole 4x8x8 slice. The times are simulated.
512 devices in a mesh: row: 8 (over z_lo, x), col: 8 (over z_hi, core), panel: 8 (over y).
Axes of the slice: x: 4, y: 8, z: 8 (z_hi: 4, z_lo: 2; z = z_hi * 2 + z_lo), core: 2. Of those that a mesh axis runs over, the one named last changes fastest.
Arguments:
- velocity: bfloat16 [4608, 6, 4096], P(('row', 'col'), None, 'panel'), may hold values from -6 to 6
- panel_weight: float32 [4096], P('panel'), may hold values from -0.109375 to 0.109375
- panel_group: int32 [4096], P('panel'), may hold values from 0 to 3
- tile_map: int32 [8, 8], replicated, may hold values from 0 to 3
- group_gain: float32 [4, 4], replicated, may hold values from 0.25 to 1
Outputs:
- qtf: float32 [4608, 2, 4608], P(('row', 'panel'), None, 'col')
All inputs are finite; a program needn't handle non-finite values.
Results may differ from a plain program's by a relative error of at most 0.0029.
Values may be sent and summed in bfloat16 or wider, within the bound.
A program may use at most 64 MiB of HBM per device.

v0:
```python
import jax
import jax.numpy as jnp
from jax import lax
from jax.sharding import PartitionSpec as P


def spread(value, axis, source):
    kept = jnp.where(lax.axis_index(axis) == source, value, 0).astype(value.dtype)
    return lax.psum(kept, axis)


def contract(left_side, right_side):
    return lax.dot_general(
        left_side, right_side, (((1,), (1,)), ((), ())), preferred_element_type=jnp.float32
    )


def pair_products(row_piece, right_side, tile_sign, half_depth):
    left_re = row_piece[:, :half_depth]
    left_im = row_piece[:, half_depth:]
    right_re = right_side[:, :half_depth]
    right_im = right_side[:, half_depth:]
    real_part = contract(left_re, right_re) + tile_sign * contract(left_im, right_im)
    imag_part = contract(left_im, right_re) - tile_sign * contract(left_re, right_im)
    return jnp.stack((real_part, imag_part), axis=1)


def local(velocity, panel_weight, panel_group, tile_map, group_gain):
    row_index = lax.axis_index("row")
    col_index = lax.axis_index("col")
    rows_block = lax.all_gather(velocity, "col", axis=0, tiled=True)
    cols_block = spread(rows_block, "row", col_index)
    chosen = (lax.broadcasted_iota(jnp.int32, tile_map.shape, 0) == row_index) & (
        lax.broadcasted_iota(jnp.int32, tile_map.shape, 1) == col_index
    )
    region = jnp.sum(jnp.where(chosen, tile_map, 0))
    group_count = group_gain.shape[0]
    case_cols = lax.broadcasted_iota(jnp.int32, group_gain.shape, 1)
    case_gains = jnp.sum(jnp.where(case_cols == region, group_gain, jnp.float32(0.0)), axis=1)
    group_ids = lax.broadcasted_iota(jnp.int32, (panel_group.shape[0], group_count), 1)
    panel_gain = jnp.sum(
        jnp.where(panel_group[:, None] == group_ids, case_gains[None, :], jnp.float32(0.0)), axis=1
    )
    panel_scale = panel_weight * panel_gain
    weighted = (rows_block.astype(jnp.float32) * panel_scale[None, None, :]).astype(jnp.bfloat16)
    tile_width = weighted.shape[0]
    slab_size = weighted.shape[2]
    left_side = weighted.reshape(tile_width, 6 * slab_size)
    right_side = cols_block.reshape(cols_block.shape[0], 6 * slab_size)
    tile_sign = jnp.where(row_index <= col_index, jnp.float32(1.0), jnp.float32(-1.0))
    half_depth = 3 * slab_size
    partial_tile = pair_products(left_side, right_side, tile_sign, half_depth)
    result = lax.psum_scatter(partial_tile, "panel", scatter_dimension=0, tiled=True)
    return result


def solution(mesh):
    return jax.shard_map(
        local,
        mesh=mesh,
        in_specs=(P(("row", "col"), None, "panel"), P("panel"), P("panel"), P(), P()),
        out_specs=P(("row", "panel"), None, "col"),
        check_vma=False,
    )
```

profile of v0, /device:TPU:1, one launch (start us, length us, event | category | flops | bytes accessed | tf_op | source)
XLA Modules:
  0.0 243.9 jit_solution(13272052365680096868)
XLA Ops:
  6.5 0.7 all-gather.2.cloned.1.call-update
  7.3 0.0 all-reduce.2.cloned.1.call-start
  7.3 59.0 %all-gather.2.cloned.1.call-done = bf16[576,6,512]{2,0,1:T(8,128)(2,1)} async-done(((bf16[72,6,512]{2,0,1:T(8,128)(2,1)}), bf16[576,6,512]{2,0,1:T(8,128)(2,1)}) %all-gather.2.cloned.1.call-update) | async-done | bytes 3538960 | tf_op jit(solution)/shard_map/all_gather | solution.py:31
  66.3 0.2 broadcast_select_fusion
  66.6 3.9 %copy.11 = bf16[576,6,512]{0,2,1:T(8,128)(2,1)} copy(bf16[576,6,512]{2,0,1:T(8,128)(2,1)S(1)} %broadcast_select_fusion) | data formatting | bytes 7077888 | tf_op jit(solution)/shard_map/jit(_where)/select_n | solution.py:8
  70.5 0.0 all-reduce.2.cloned.1.call-update
  70.5 0.0 reduce-scatter.2.cloned.1.call-start
  70.6 0.6 copy-done.2
  71.2 0.7 select_reduce_fusion.1
  71.9 0.6 iota_compare_fusion.3
  72.5 0.1 select_reduce_fusion.2
  72.6 0.1 select_reduce_fusion
  72.8 2.6 %multiply_convert_fusion = bf16[576,6,512]{2,0,1:T(8,128)(2,1)} fusion(bf16[576,6,512]{2,0,1:T(8,128)(2,1)S(1)} %copy-done, f32[512]{0:T(512)S(1)} %mul.21), kind=kLoop, calls=%fused_computation | loop fusion | flops 5308416 | bytes 7079936 | tf_op jit(solution)/shard_map/convert_element_type | solution.py:45
  75.3 5.9 %copy.10 = bf16[576,6,512]{0,2,1:T(8,128)(2,1)} copy(bf16[576,6,512]{2,0,1:T(8,128)(2,1)} %multiply_convert_fusion) | data formatting | bytes 7077888 | tf_op jit(solution)/shard_map/convert_element_type | solution.py:45
  81.3 99.7 %all-reduce.2.cloned.1.call-done = bf16[576,3072]{0,1:T(8,128)(2,1)} async-done(((bf16[576,3072]{0,1:T(8,128)(2,1)}), bf16[576,3072]{0,1:T(8,128)(2,1)}) %all-reduce.2.cloned.1.call-update) | async-done | bytes 3538960 | tf_op jit(solution)/shard_map/psum | solution.py:9
  181.0 3.9 %fusion = f32[576,576]{1,0:T(8,128)S(1)} fusion(bf16[576,3072]{0,1:T(8,128)(2,1)} %all-reduce.2.cloned.1.call-done, bf16[576,3072]{0,1:T(8,128)(2,1)} %bitcast.7), kind=kOutput, calls=%fused_computation.3 | convolution fusion | flops 1019215872 | bytes 5259264 | tf_op jit(solution)/shard_map/dot_general | solution.py:13
  184.8 0.6 copy-done.6
  185.4 1.6 fusion.2
  187.0 1.6 subtract_bitcast_fusion
  188.6 1.6 add_bitcast_fusion
  190.2 1.8 pad_maximum_fusion
  192.0 0.0 reduce-scatter.2.cloned.1.call-update
  192.0 43.4 %reduce-scatter.2.cloned.1.call-done = f32[72,2,576]{2,0,1:T(8,128)} async-done(((f32[576,2,576]{2,0,1:T(8,128)}), f32[72,2,576]{2,0,1:T(8,128)}) %reduce-scatter.2.cloned.1.call-update) | async-done | bytes 331792 | tf_op jit(solution)/shard_map/reduce_scatter | solution.py:53
  235.5 1.9 copy.12
  (15 shorter events, 0.0 us)
Async XLA Ops:
  6.5 59.8 %all-gather.2.cloned.1.call-start = ((), (), s32[]{:S(2)}) async-start(), calls=%async_computation.1 | async-start | bytes 3981312 | tf_op jit(solution)/shard_map/all_gather | solution.py:31
  7.3 173.7 %all-reduce.2.cloned.1.call-start = ((), (), s32[]{:S(2)}) async-start(), calls=%async_computation.2 | async-start | bytes 7864320 | tf_op jit(solution)/shard_map/psum | solution.py:9
  70.5 0.7 copy-start.2
  70.5 2.0 copy-start.4
  70.5 2.2 copy-start.5
  70.5 2.3 copy-start.3
  70.5 2.3 copy-start
  70.5 165.0 %reduce-scatter.2.cloned.1.call-start = ((), (), s32[]{:S(2)}) async-start(), calls=%async_computation.3 | async-start | bytes 3317760 | tf_op jit(solution)/shard_map/reduce_scatter | solution.py:53
  180.9 3.9 %copy-start.1 = (bf16[576,6,512]{0,2,1:T(8,128)(2,1)S(1)}, bf16[576,6,512]{0,2,1:T(8,128)(2,1)}, u32[]{:S(2)}) copy-start(bf16[576,6,512]{0,2,1:T(8,128)(2,1)} %copy.10) | copy-start | bytes 10616836
  181.0 4.5 %copy-start.6 = (bf16[576,3072]{0,1:T(8,128)(2,1)S(1)}, bf16[576,3072]{0,1:T(8,128)(2,1)}, u32[]{:S(2)}) copy-start(bf16[576,3072]{0,1:T(8,128)(2,1)} %all-reduce.2.cloned.1.call-done) | copy-start | bytes 10616836
Sparse Core Ops, SparseCore 0:
  9.5 56.8 all-gather.1
  70.6 110.2 all-reduce.1
  192.2 43.2 reduce-scatter.1
where the time goes:
time: 247 us; the launch traced here: 244 us
  waiting for transfers between devices  203 us (82%)
  between operations  13.2 us (5%)
  local copies, waits for them, and re-layouts  12.9 us (5%)
  matrix products  8.64 us (3%)
  other arithmetic  6.18 us (3%)
    psum x1, waiting for transfers between devices, spread(): return lax.psum(kept, axis)  99.7 us
    all_gather x1, waiting for transfers between devices, local(): rows_block = lax.all_gather(velocity, 'col', axis=0, tiled=True)  59 us
    reduce_scatter x1, waiting for transfers between devices, local(): lax.psum_scatter(partial_tile, 'panel', scatter_dimension=0, tiled=True)  43.4 us
    dot_general x4, matrix products, contract(): lax.dot_general(left_side, right_side, (((1,), (1,)), ((), ())), preferre...  8.64 us
    convert_element_type x1, local copies, waits for them, and re-layouts, local(): (rows_block.astype(jnp.float32) * panel_scale[None, None, :]).astype(jnp....  5.93 us
  transfers between devices with their start and end apart: 3, of which 3 were waited for; matrix products, arithmetic and copies ran while one was open for 4% of the time, Pallas kernels for 0%

commit v1 on v0

v1 whole, which is shorter than its diff:
```python
import functools

import jax
import jax.numpy as jnp
from jax import lax
from jax.experimental import pallas as pl
from jax.experimental.pallas import tpu as pltpu
from jax.sharding import PartitionSpec as P

MESH = pl.DeviceIdType.MESH
NX = 4
NZ = 8
NY = 8


def device(x, z, core, y):
    return (lax.rem(z, 2) * NX + x, (z // 2) * 2 + core, y)


def kernel(
    v_ref, weight_ref, group_ref, case_ref, gain_ref, out_ref,
    rbuf, cbuf, scale, coef, acc, tbuf, ybuf, unit, piece, obuf,
    rsem, csem, ysem, osem, own_sem, near_sem, far_sem, cown_sem, cfwd_sem,
    part_sem, ysend_sem, osend_sem, local_sem,
):
    rows = v_ref.shape[1] // 2
    pair_rows = 4 * rows
    row, col, y = lax.axis_index("row"), lax.axis_index("col"), lax.axis_index("panel")
    zl, x = row // NX, lax.rem(row, NX)
    zh, core = col // 2, lax.rem(col, 2)
    z = 2 * zh + zl
    odd = lax.rem(zl + core, 2)
    tile_row = NX * core + x
    near = 2 - odd

    def chip_z(offset):
        return lax.rem(z + offset + NZ, NZ)

    def chip_x(offset):
        return lax.rem(x + offset + NX, NX)

    def final_owner(k):
        return (tile_row, NX * zl + k, y)

    is_final_self = jnp.logical_and(core == zl, col // NX == zl)
    final_self = lax.rem(col, NX)

    barrier = pltpu.get_barrier_semaphore()

    def greet(target):
        pl.semaphore_signal(barrier, inc=1, device_id=target, device_id_type=MESH)

    for dirn in (1, -1):
        for k in range(2):
            greet(device(x, chip_z(dirn), k, y))
        greet(device(chip_x(dirn), z, core, y))
    greet(device(x, z, 1 - core, y))
    for step in range(1, NY):
        greet((row, col, lax.rem(y + step, NY)))
    for h in range(NZ // 2):
        source_row = NX * (col // NX) + x
        source_col = 2 * h + zl
        @pl.when(jnp.logical_not(jnp.logical_and(is_final_self, h == zh)))
        def _():
            greet((source_row, source_col, y))
    pl.semaphore_wait(barrier, 18 - jnp.where(is_final_self, 1, 0))

    def remote(src, dst, send, recv, target):
        return pltpu.make_async_remote_copy(
            src_ref=src, dst_ref=dst, send_sem=send, recv_sem=recv,
            device_id=target, device_id_type=MESH,
        )

    def own_copy(target, c):
        where = (chip_z(1), chip_z(-1), z)[target]
        to = zl if target < 2 else 1 - core
        return remote(
            v_ref.at[c], rbuf.at[zh, c, core], own_sem.at[target, c],
            rsem.at[zh, c, core], device(x, where, to, y),
        )

    def cown_copy(target):
        to = device(chip_x(1 - 2 * target), z, core, y)
        return remote(v_ref, cbuf.at[x, :, core], cown_sem.at[target], csem.at[x, core], to)

    def part_copy(offset):
        src = v_ref if offset == 0 else cbuf.at[chip_x(offset), :, core]
        return remote(
            src, cbuf.at[chip_x(offset), :, core], part_sem.at[offset],
            csem.at[chip_x(offset), core], device(x, z, 1 - core, y),
        )

    local_c = pltpu.make_async_copy(v_ref, cbuf.at[x, :, core], local_sem.at[0])
    local_r = pltpu.make_async_copy(v_ref, rbuf.at[zh, :, core], local_sem.at[1])
    for c in range(3):
        own_copy(0, c).start()
        own_copy(1, c).start()
        if c == 0:
            cown_copy(0).start()
            cown_copy(1).start()
    part_copy(0).start()
    @pl.when(odd == 1)
    def _():
        for c in range(3):
            own_copy(2, c).start()
    local_c.start()
    @pl.when(odd == 0)
    def _():
        local_r.start()

    lanes = lax.broadcasted_iota(jnp.int32, (1, coef.shape[1]), 1)
    imag = lanes < 0
    for m in range(8):
        lo = m * 2 * rows + rows
        imag = jnp.logical_or(imag, jnp.logical_and(lanes >= lo, lanes < lo + rows))
    sign = jnp.zeros(lanes.shape, jnp.float32)
    for k in range(NX):
        tile_col = NX * zl + k
        case = case_ref[tile_row, tile_col]
        groups = group_ref[...]
        gain = jnp.zeros(groups.shape, jnp.float32)
        for g in range(gain_ref.shape[0]):
            gain = jnp.where(groups == g, gain_ref[g, case], gain)
        scale[pl.ds(k, 1), :] = weight_ref[...] * gain
        tile_sign = jnp.where(tile_row <= tile_col, 1.0, -1.0).astype(jnp.float32)
        sign = jnp.where(lanes >= pair_rows * k, tile_sign, sign)
    coef[pl.ds(0, 1), :] = jnp.where(imag, -sign, 1.0)
    coef[pl.ds(1, 1), :] = jnp.where(imag, 1.0, sign)

    def slot(offset):
        return chip_z(offset) // 2

    def arrival(h, c, k):
        return remote(
            rbuf.at[h, c, k], rbuf.at[h, c, k], own_sem.at[0, 0], rsem.at[h, c, k],
            device(x, chip_z(1), core, y),
        )

    def near_copy(side, c, k):
        dirn = 1 - 2 * side
        h = slot(-dirn * near)
        return remote(
            rbuf.at[h, c, k], rbuf.at[h, c, k], near_sem.at[side, c, k],
            rsem.at[h, c, k], device(x, chip_z(dirn), core, y),
        )

    def far_copy(side, c):
        dirn = 1 - 2 * side
        h = slot(-dirn * 3)
        return remote(
            rbuf.at[h, c, side], rbuf.at[h, c, side], far_sem.at[side, c],
            rsem.at[h, c, side], device(x, chip_z(dirn), core, y),
        )

    def near_step(c):
        for k in range(2):
            for side in range(2):
                arrival(slot((2 * side - 1) * near), c, k).wait_recv()
                near_copy(side, c, k).start()

    def far_step(c):
        for k in range(2):
            for side in range(2):
                arrival(slot((2 * side - 1) * 3), c, k).wait_recv()
                if k == side:
                    far_copy(side, c).start()

    def c_arrival(k, which):
        return remote(
            cbuf.at[k, :, which], cbuf.at[k, :, which], own_sem.at[0, 0],
            csem.at[k, which], device(x, z, 1 - core, y),
        )

    back = 2 * core - 1
    cfwd = remote(
        cbuf.at[chip_x(back), :, core], cbuf.at[chip_x(back), :, core], cfwd_sem.at[0],
        csem.at[chip_x(back), core], device(chip_x(-back), z, core, y),
    )

    @pl.when(odd == 1)
    def _():
        for c in range(3):
            near_step(c)
    c_arrival(chip_x(back), core).wait_recv()
    cfwd.start()
    c_arrival(chip_x(-back), core).wait_recv()
    part_copy(1).start()
    part_copy(3).start()
    @pl.when(odd == 0)
    def _():
        near_step(0)
    c_arrival(chip_x(2), core).wait_recv()
    part_copy(2).start()
    for offset in range(NX):
        c_arrival(chip_x(offset), 1 - core).wait_recv()
    local_c.wait()
    @pl.when(odd == 0)
    def _():
        local_r.wait()

    def pair_slot(pair):
        even_offset = 2 * (lax.rem(pair + pair // 2, 4) + 2 * (pair // 3))
        odd_offset = (2 * lax.rem(pair, 2) - 1) * (1 + 2 * (pair // 2))
        return slot(jnp.where(odd == 1, odd_offset, even_offset))

    def ysend(pair, k, p):
        return remote(
            tbuf.at[pair, k], ybuf.at[y], ysend_sem.at[pair, k], ysem.at[y], (row, col, p)
        )

    def finish(pair):
        h = pair_slot(pair)
        for k in range(2):
            base = k * 2 * rows
            top = jnp.concatenate([acc[j, base:base + rows, :] for j in range(NX)], axis=1)
            low = jnp.concatenate([acc[j, base + rows:base + 2 * rows, :] for j in range(NX)], axis=1)
            width = low.shape[1]
            swapped = jnp.where(
                imag, pltpu.roll(low, rows, 1), pltpu.roll(low, width - rows, 1)
            )
            total = coef[pl.ds(0, 1), :] * top + coef[pl.ds(1, 1), :] * swapped
            p = 2 * h + k
            @pl.when(p == y)
            def _():
                unit[...] = total
            @pl.when(p != y)
            def _():
                tbuf[pair, k] = total.astype(jnp.bfloat16)
                ysend(pair, k, p).start()

    def y_arrival(source):
        return remote(
            ybuf.at[source], ybuf.at[source], own_sem.at[0, 0], ysem.at[source],
            (row, col, lax.rem(y + 1, NY)),
        )

    def osend(k):
        return remote(
            piece.at[k], obuf.at[zh], osend_sem.at[k], osem.at[zh], final_owner(k)
        )

    def is_self(k):
        return jnp.logical_and(is_final_self, final_self == k)

    def reduce_unit():
        total = unit[...]
        for step in range(1, NY):
            source = lax.rem(y + step, NY)
            y_arrival(source).wait_recv()
            total = total + ybuf[source].astype(jnp.float32)
        for k in range(NX):
            part = total[:, k * pair_rows:(k + 1) * pair_rows]
            piece[k] = part
            @pl.when(is_self(k))
            def _():
                obuf[zh] = part
            @pl.when(jnp.logical_not(is_self(k)))
            def _():
                osend(k).start()

    my_h = y // 2

    def step_body(n, carry):
        pair, c = n // 3, lax.rem(n, 3)
        @pl.when(odd == 0)
        def _():
            @pl.when(pair == 0)
            def _():
                arrival(zh, c, 1 - core).wait_recv()
            @pl.when(jnp.logical_and(pair == 0, c > 0))
            def _():
                near_step(c)
            @pl.when(pair == 3)
            def _():
                for k in range(2):
                    arrival(slot(4), c, k).wait_recv()
        @pl.when(jnp.logical_and(odd == 1, pair == 2))
        def _():
            far_step(c)
        left = rbuf[pair_slot(pair), c].reshape(pair_rows, v_ref.shape[2]).astype(jnp.float32)
        for k in range(NX):
            weighted = (left * scale[pl.ds(k, 1), :]).astype(jnp.bfloat16)
            right = cbuf[k, c].reshape(pair_rows, v_ref.shape[2])
            product = lax.dot_general(
                weighted, right, (((1,), (1,)), ((), ())), preferred_element_type=jnp.float32
            )
            @pl.when(c == 0)
            def _():
                acc[k] = product
            @pl.when(c > 0)
            def _():
                acc[k] = acc[k] + product
        @pl.when(c == 2)
        def _():
            finish(pair)
            @pl.when(jnp.logical_or(
                jnp.logical_and(pair == 2, pair_slot(0) == my_h),
                jnp.logical_and(pair == 2, pair_slot(1) == my_h),
            ))
            def _():
                reduce_unit()
        return carry

    lax.fori_loop(0, 12, step_body, 0)
    @pl.when(jnp.logical_or(pair_slot(2) == my_h, pair_slot(3) == my_h))
    def _():
        reduce_unit()

    for h in range(NZ // 2):
        @pl.when(jnp.logical_not(jnp.logical_and(is_final_self, h == zh)))
        def _():
            remote(
                obuf.at[h], obuf.at[h], own_sem.at[0, 0], osem.at[h],
                device(x, z, 1 - core, y),
            ).wait_recv()
    got = [obuf[h] for h in range(NZ // 2)]
    for ri in range(2):
        out_ref[ri] = jnp.concatenate(
            [got[h][:, (2 * k + ri) * rows:(2 * k + ri + 1) * rows]
             for h in range(NZ // 2) for k in range(2)],
            axis=1,
        )

    for c in range(3):
        own_copy(0, c).wait_send()
        own_copy(1, c).wait_send()
        for side in range(2):
            for k in range(2):
                near_copy(side, c, k).wait_send()
    @pl.when(odd == 1)
    def _():
        for c in range(3):
            own_copy(2, c).wait_send()
            for side in range(2):
                far_copy(side, c).wait_send()
    cown_copy(0).wait_send()
    cown_copy(1).wait_send()
    cfwd.wait_send()
    for offset in range(NX):
        part_copy(offset).wait_send()
    for pair in range(4):
        for k in range(2):
            p = 2 * pair_slot(pair) + k
            @pl.when(p != y)
            def _():
                ysend(pair, k, p).wait_send()
    for k in range(NX):
        @pl.when(jnp.logical_not(is_self(k)))
        def _():
            osend(k).wait_send()


def local(velocity, panel_weight, panel_group, tile_map, group_gain):
    columns, parts, slab = velocity.shape
    half = parts // 2
    blocks = velocity.reshape(columns, 2, half, slab).transpose(2, 1, 0, 3)
    blocks = blocks.reshape(half, 2 * columns, slab)
    block = (half, 2, 2 * columns, slab)
    pair_rows = 4 * columns
    vmem = pl.BlockSpec(memory_space=pltpu.VMEM)
    smem = pl.BlockSpec(memory_space=pltpu.SMEM)
    dma = pltpu.SemaphoreType.DMA
    result = pl.pallas_call(
        kernel,
        out_shape=jax.ShapeDtypeStruct((2, columns, 8 * columns), jnp.float32),
        in_specs=[vmem, vmem, vmem, smem, smem],
        out_specs=vmem,
        scratch_shapes=[
            pltpu.VMEM((NZ // 2,) + block, jnp.bfloat16),
            pltpu.VMEM((NX,) + block, jnp.bfloat16),
            pltpu.VMEM((NX, slab), jnp.float32),
            pltpu.VMEM((2, NX * pair_rows), jnp.float32),
            pltpu.VMEM((NX, pair_rows, pair_rows), jnp.float32),
            pltpu.VMEM((4, 2, columns, NX * pair_rows), jnp.bfloat16),
            pltpu.VMEM((NY, columns, NX * pair_rows), jnp.bfloat16),
            pltpu.VMEM((columns, NX * pair_rows), jnp.float32),
            pltpu.VMEM((NX, columns, pair_rows), jnp.float32),
            pltpu.VMEM((NZ // 2, columns, pair_rows), jnp.float32),
            dma((NZ // 2, 3, 2)),
            dma((NX, 2)),
            dma((NY,)),
            dma((NZ // 2,)),
            dma((3, 3)),
            dma((2, 3, 2)),
            dma((2, 3)),
            dma((2,)),
            dma((1,)),
            dma((NX,)),
            dma((4, 2)),
            dma((NX,)),
            dma((2,)),
        ],
        compiler_params=pltpu.CompilerParams(
            collective_id=0, has_side_effects=True, vmem_limit_bytes=40 * 1024 * 1024
        ),
    )(blocks, panel_weight[None, :], panel_group[None, :], tile_map, group_gain)
    return result.transpose(1, 0, 2)


def solution(mesh):
    return jax.shard_map(
        local,
        mesh=mesh,
        in_specs=(P(("row", "col"), None, "panel"), P("panel"), P("panel"), P(), P()),
        out_specs=P(("row", "panel"), None, "col"),
        check_vma=False,
    )
```

time: 247 us -> 101 us (0.41)
  the two profiles are of different devices: /device:TPU:1 before, /device:TPU:105 now
where the time goes in v1:
time: 101 us
  Pallas kernels  99 us (98%)
  local copies, waits for them, and re-layouts  2.03 us (2%)
    pallas_call x1, Pallas kernels, local(): pl.pallas_call(kernel, out_shape=jax.ShapeDtypeStruct((2, columns, 8 * co...  99 us

profile of v1, /device:TPU:105, one launch (start us, length us, event | category | flops | bytes accessed | tf_op | source)
XLA Modules:
  0.0 101.1 jit_solution(15809324160218315155)
XLA Ops:
  0.0 0.0 copy-start
  0.0 0.0 copy-start.1
  0.0 0.0 copy-start.2
  0.0 0.0 copy-start.3
  0.0 1.1 %copy.6 = bf16[72,2,3,512]{3,0,1,2:T(8,128)(2,1)S(1)} copy(bf16[72,2,3,512]{3,0,2,1:T(8,128)(2,1)} %bitcast.11) | data formatting | bytes 884736 | tf_op jit(solution)/shard_map/reshape | solution.py:356
  1.1 0.0 copy-done
  1.1 0.0 copy-done.1
  1.1 0.0 copy-done.2
  1.1 0.0 copy-done.3
  1.2 99.0 %shard_map.55 = f32[2,72,576]{2,1,0:T(8,128)S(1)} custom-call(bf16[3,144,512]{2,1,0:T(8,128)(2,1)S(1)} %bitcast.7, f32[1,512]{1,0:T(1,128)S(1)} %bitcast.9, s32[1,512]{1,0:T(1,128)S(1)} %bitcast.10, s32[8,8]{1,0:T(8,128)S(1)} %copy-done, f32[4,4]{1,0:T(4,128)S(1)} %copy-done.3), custom_call_target="tpu_custom_call" | custom-call | tf_op jit(solution)/shard_map/pallas_call | solution.py:363
  100.1 0.9 copy.7
Async XLA Ops:
  0.0 1.1 %copy-start = (s32[8,8]{1,0:T(8,128)S(1)}, s32[8,8]{1,0:T(8,128)}, u32[]{:S(2)}) copy-start(s32[8,8]{1,0:T(8,128)} %case_ref.1) | copy-start | bytes 772
  0.0 1.1 %copy-start.1 = (f32[512]{0:T(512)S(1)}, f32[512]{0:T(512)}, u32[]{:S(2)}) copy-start(f32[512]{0:T(512)} %param.6) | copy-start | bytes 6148
  0.0 1.1 %copy-start.2 = (s32[512]{0:T(512)S(1)}, s32[512]{0:T(512)}, u32[]{:S(2)}) copy-start(s32[512]{0:T(512)} %param.7) | copy-start | bytes 6148
  0.0 1.1 %copy-start.3 = (f32[4,4]{1,0:T(4,128)S(1)}, f32[4,4]{1,0:T(4,128)}, u32[]{:S(2)}) copy-start(f32[4,4]{1,0:T(4,128)} %gain_ref.1) | copy-start | bytes 196

commit v2 on v1

--- a/solution.py
+++ b/solution.py
@@ -19,7 +19,7 @@
 
 def kernel(
     v_ref, weight_ref, group_ref, case_ref, gain_ref, out_ref,
-    rbuf, cbuf, scale, coef, acc, tbuf, ybuf, unit, piece, obuf,
+    rbuf, cbuf, scale, coef, acc, own, tbuf, ybuf, piece, obuf,
     rsem, csem, ysem, osem, own_sem, near_sem, far_sem, cown_sem, cfwd_sem,
     part_sem, ysend_sem, osend_sem, local_sem,
 ):
@@ -55,7 +55,7 @@
             greet(device(x, chip_z(dirn), k, y))
         greet(device(chip_x(dirn), z, core, y))
     greet(device(x, z, 1 - core, y))
-    for step in range(1, NY):
+    for step in (1, NY - 1):
         greet((row, col, lax.rem(y + step, NY)))
     for h in range(NZ // 2):
         source_row = NX * (col // NX) + x
@@ -63,7 +63,7 @@
         @pl.when(jnp.logical_not(jnp.logical_and(is_final_self, h == zh)))
         def _():
             greet((source_row, source_col, y))
-    pl.semaphore_wait(barrier, 18 - jnp.where(is_final_self, 1, 0))
+    pl.semaphore_wait(barrier, 13 - jnp.where(is_final_self, 1, 0))
 
     def remote(src, dst, send, recv, target):
         return pltpu.make_async_remote_copy(
@@ -79,15 +79,18 @@
             rsem.at[zh, c, core], device(x, where, to, y),
         )
 
-    def cown_copy(target):
+    def cown_copy(target, c):
         to = device(chip_x(1 - 2 * target), z, core, y)
-        return remote(v_ref, cbuf.at[x, :, core], cown_sem.at[target], csem.at[x, core], to)
-
-    def part_copy(offset):
-        src = v_ref if offset == 0 else cbuf.at[chip_x(offset), :, core]
-        return remote(
-            src, cbuf.at[chip_x(offset), :, core], part_sem.at[offset],
-            csem.at[chip_x(offset), core], device(x, z, 1 - core, y),
+        return remote(
+            v_ref.at[c], cbuf.at[x, c, core], cown_sem.at[target, c], csem.at[x, c, core], to
+        )
+
+    def part_copy(offset, c):
+        k = chip_x(offset)
+        src = v_ref.at[c] if offset == 0 else cbuf.at[k, c, core]
+        return remote(
+            src, cbuf.at[k, c, core], part_sem.at[offset, c], csem.at[k, c, core],
+            device(x, z, 1 - core, y),
         )
 
     local_c = pltpu.make_async_copy(v_ref, cbuf.at[x, :, core], local_sem.at[0])
@@ -95,13 +98,11 @@
     for c in range(3):
         own_copy(0, c).start()
         own_copy(1, c).start()
-        if c == 0:
-            cown_copy(0).start()
-            cown_copy(1).start()
-    part_copy(0).start()
-    @pl.when(odd == 1)
-    def _():
-        for c in range(3):
+        cown_copy(0, c).start()
+        cown_copy(1, c).start()
+        part_copy(0, c).start()
+        @pl.when(odd == 1)
+        def _():
             own_copy(2, c).start()
     local_c.start()
     @pl.when(odd == 0)
@@ -165,34 +166,32 @@
                 if k == side:
                     far_copy(side, c).start()
 
-    def c_arrival(k, which):
-        return remote(
-            cbuf.at[k, :, which], cbuf.at[k, :, which], own_sem.at[0, 0],
-            csem.at[k, which], device(x, z, 1 - core, y),
+    def c_arrival(k, c, which):
+        return remote(
+            cbuf.at[k, c, which], cbuf.at[k, c, which], own_sem.at[0, 0],
+            csem.at[k, c, which], device(x, z, 1 - core, y),
         )
 
     back = 2 * core - 1
-    cfwd = remote(
-        cbuf.at[chip_x(back), :, core], cbuf.at[chip_x(back), :, core], cfwd_sem.at[0],
-        csem.at[chip_x(back), core], device(chip_x(-back), z, core, y),
-    )
-
-    @pl.when(odd == 1)
-    def _():
-        for c in range(3):
-            near_step(c)
-    c_arrival(chip_x(back), core).wait_recv()
-    cfwd.start()
-    c_arrival(chip_x(-back), core).wait_recv()
-    part_copy(1).start()
-    part_copy(3).start()
-    @pl.when(odd == 0)
-    def _():
-        near_step(0)
-    c_arrival(chip_x(2), core).wait_recv()
-    part_copy(2).start()
-    for offset in range(NX):
-        c_arrival(chip_x(offset), 1 - core).wait_recv()
+
+    def cfwd_copy(c):
+        k = chip_x(back)
+        return remote(
+            cbuf.at[k, c, core], cbuf.at[k, c, core], cfwd_sem.at[c],
+            csem.at[k, c, core], device(chip_x(-back), z, core, y),
+        )
+
+    def c_step(c):
+        c_arrival(chip_x(back), c, core).wait_recv()
+        cfwd_copy(c).start()
+        c_arrival(chip_x(-back), c, core).wait_recv()
+        part_copy(1, c).start()
+        part_copy(3, c).start()
+        c_arrival(chip_x(2), c, core).wait_recv()
+        part_copy(2, c).start()
+        for offset in range(NX):
+            c_arrival(chip_x(offset), c, 1 - core).wait_recv()
+
     local_c.wait()
     @pl.when(odd == 0)
     def _():
@@ -203,13 +202,32 @@
         odd_offset = (2 * lax.rem(pair, 2) - 1) * (1 + 2 * (pair // 2))
         return slot(jnp.where(odd == 1, odd_offset, even_offset))
 
-    def ysend(pair, k, p):
-        return remote(
-            tbuf.at[pair, k], ybuf.at[y], ysend_sem.at[pair, k], ysem.at[y], (row, col, p)
+    third = own.shape[3]
+
+    def role(pair, k):
+        delta = lax.rem(y - (2 * pair_slot(pair) + k) + NY, NY)
+        longest = NY // 2 - k
+        down = delta <= longest
+        stage = jnp.where(down, longest - delta, delta - (longest + 1))
+        return delta, down, stage
+
+    def ysend(pair, k, q):
+        delta, down, _ = role(pair, k)
+        unit = 2 * pair + k
+        there = jnp.where(delta == NY - 1, NY, unit)
+        to = lax.rem(y + jnp.where(down, NY - 1, 1), NY)
+        return remote(
+            tbuf.at[unit, q], ybuf.at[there, q], ysend_sem.at[unit, q], ysem.at[there, q],
+            (row, col, to),
+        )
+
+    def y_arrival(unit, q):
+        return remote(
+            ybuf.at[unit, q], ybuf.at[unit, q], own_sem.at[0, 0], ysem.at[unit, q],
+            (row, col, lax.rem(y + 1, NY)),
         )
 
     def finish(pair):
-        h = pair_slot(pair)
         for k in range(2):
             base = k * 2 * rows
             top = jnp.concatenate([acc[j, base:base + rows, :] for j in range(NX)], axis=1)
@@ -219,20 +237,30 @@
                 imag, pltpu.roll(low, rows, 1), pltpu.roll(low, width - rows, 1)
             )
             total = coef[pl.ds(0, 1), :] * top + coef[pl.ds(1, 1), :] * swapped
-            p = 2 * h + k
-            @pl.when(p == y)
-            def _():
-                unit[...] = total
-            @pl.when(p != y)
-            def _():
-                tbuf[pair, k] = total.astype(jnp.bfloat16)
-                ysend(pair, k, p).start()
-
-    def y_arrival(source):
-        return remote(
-            ybuf.at[source], ybuf.at[source], own_sem.at[0, 0], ysem.at[source],
-            (row, col, lax.rem(y + 1, NY)),
-        )
+            delta, _, stage = role(pair, k)
+            unit = 2 * pair + k
+            is_head = jnp.logical_and(delta > 0, stage == 0)
+            @pl.when(is_head)
+            def _():
+                for q in range(3):
+                    tbuf[unit, q] = total[:, q * third:(q + 1) * third].astype(jnp.bfloat16)
+                    ysend(pair, k, q).start()
+            @pl.when(jnp.logical_not(is_head))
+            def _():
+                for q in range(3):
+                    own[unit, q] = total[:, q * third:(q + 1) * third]
+
+    def relay(pair, when):
+        for k in range(2):
+            delta, _, stage = role(pair, k)
+            unit = 2 * pair + k
+            @pl.when(jnp.logical_and(delta > 0, stage == when))
+            def _():
+                for q in range(3):
+                    y_arrival(unit, q).wait_recv()
+                    sums = own[unit, q] + ybuf[unit, q].astype(jnp.float32)
+                    tbuf[unit, q] = sums.astype(jnp.bfloat16)
+                    ysend(pair, k, q).start()
 
     def osend(k):
         return remote(
@@ -242,12 +270,16 @@
     def is_self(k):
         return jnp.logical_and(is_final_self, final_self == k)
 
-    def reduce_unit():
-        total = unit[...]
-        for step in range(1, NY):
-            source = lax.rem(y + step, NY)
-            y_arrival(source).wait_recv()
-            total = total + ybuf[source].astype(jnp.float32)
+    def reduce_unit(pair):
+        unit = 2 * pair + lax.rem(y, 2)
+        parts = []
+        for q in range(3):
+            y_arrival(unit, q).wait_recv()
+            y_arrival(NY, q).wait_recv()
+            parts.append(
+                own[unit, q] + ybuf[unit, q].astype(jnp.float32) + ybuf[NY, q].astype(jnp.float32)
+            )
+        total = jnp.concatenate(parts, axis=1)
         for k in range(NX):
             part = total[:, k * pair_rows:(k + 1) * pair_rows]
             piece[k] = part
@@ -258,22 +290,27 @@
             def _():
                 osend(k).start()
 
-    my_h = y // 2
+    def holds(pair):
+        return pair_slot(pair) == y // 2
 
     def step_body(n, carry):
         pair, c = n // 3, lax.rem(n, 3)
-        @pl.when(odd == 0)
-        def _():
-            @pl.when(pair == 0)
-            def _():
-                arrival(zh, c, 1 - core).wait_recv()
-            @pl.when(jnp.logical_and(pair == 0, c > 0))
-            def _():
-                near_step(c)
-            @pl.when(pair == 3)
-            def _():
-                for k in range(2):
-                    arrival(slot(4), c, k).wait_recv()
+        @pl.when(jnp.logical_or(jnp.logical_and(odd == 1, pair == 0), jnp.logical_and(odd == 0, n == 2)))
+        def _():
+            near_step(odd * n)
+        @pl.when(pair == 0)
+        def _():
+            c_step(c)
+        @pl.when(jnp.logical_and(odd == 0, jnp.logical_or(n == 2, n == 4)))
+        def _():
+            near_step(n // 2)
+        @pl.when(jnp.logical_and(odd == 0, pair == 0))
+        def _():
+            arrival(zh, c, 1 - core).wait_recv()
+        @pl.when(jnp.logical_and(odd == 0, pair == 3))
+        def _():
+            for k in range(2):
+                arrival(slot(4), c, k).wait_recv()
         @pl.when(jnp.logical_and(odd == 1, pair == 2))
         def _():
             far_step(c)
@@ -293,18 +330,27 @@
         @pl.when(c == 2)
         def _():
             finish(pair)
-            @pl.when(jnp.logical_or(
-                jnp.logical_and(pair == 2, pair_slot(0) == my_h),
-                jnp.logical_and(pair == 2, pair_slot(1) == my_h),
-            ))
-            def _():
-                reduce_unit()
+        @pl.when(pair > 0)
+        def _():
+            relay(pair - 1, c + 1)
+        @pl.when(jnp.logical_and(jnp.logical_and(pair > 1, c == 0), holds(pair - 2)))
+        def _():
+            reduce_unit(pair - 2)
         return carry
 
     lax.fori_loop(0, 12, step_body, 0)
-    @pl.when(jnp.logical_or(pair_slot(2) == my_h, pair_slot(3) == my_h))
+
+    def tail_body(n, carry):
+        relay(3, n + 1)
+        @pl.when(jnp.logical_and(n == 0, holds(2)))
+        def _():
+            reduce_unit(2)
+        return carry
+
+    lax.fori_loop(0, 3, tail_body, 0)
+    @pl.when(holds(3))
     def _():
-        reduce_unit()
+        reduce_unit(3)
 
     for h in range(NZ // 2):
         @pl.when(jnp.logical_not(jnp.logical_and(is_final_self, h == zh)))
@@ -333,17 +379,18 @@
             own_copy(2, c).wait_send()
             for side in range(2):
                 far_copy(side, c).wait_send()
-    cown_copy(0).wait_send()
-    cown_copy(1).wait_send()
-    cfwd.wait_send()
-    for offset in range(NX):
-        part_copy(offset).wait_send()
+    for c in range(3):
+        cown_copy(0, c).wait_send()
+        cown_copy(1, c).wait_send()
+        cfwd_copy(c).wait_send()
+        for offset in range(NX):
+            part_copy(offset, c).wait_send()
     for pair in range(4):
         for k in range(2):
-            p = 2 * pair_slot(pair) + k
-            @pl.when(p != y)
-            def _():
-                ysend(pair, k, p).wait_send()
+            @pl.when(role(pair, k)[0] > 0)
+            def _():
+                for q in range(3):
+                    ysend(pair, k, q).wait_send()
     for k in range(NX):
         @pl.when(jnp.logical_not(is_self(k)))
         def _():
@@ -357,6 +404,7 @@
     blocks = blocks.reshape(half, 2 * columns, slab)
     block = (half, 2, 2 * columns, slab)
     pair_rows = 4 * columns
+    third = NX * pair_rows // 3
     vmem = pl.BlockSpec(memory_space=pltpu.VMEM)
     smem = pl.BlockSpec(memory_space=pltpu.SMEM)
     dma = pltpu.SemaphoreType.DMA
@@ -371,22 +419,22 @@
             pltpu.VMEM((NX, slab), jnp.float32),
             pltpu.VMEM((2, NX * pair_rows), jnp.float32),
             pltpu.VMEM((NX, pair_rows, pair_rows), jnp.float32),
-            pltpu.VMEM((4, 2, columns, NX * pair_rows), jnp.bfloat16),
-            pltpu.VMEM((NY, columns, NX * pair_rows), jnp.bfloat16),
-            pltpu.VMEM((columns, NX * pair_rows), jnp.float32),
+            pltpu.VMEM((NY, 3, columns, third), jnp.float32),
+            pltpu.VMEM((NY, 3, columns, third), jnp.bfloat16),
+            pltpu.VMEM((NY + 1, 3, columns, third), jnp.bfloat16),
             pltpu.VMEM((NX, columns, pair_rows), jnp.float32),
             pltpu.VMEM((NZ // 2, columns, pair_rows), jnp.float32),
             dma((NZ // 2, 3, 2)),
-            dma((NX, 2)),
-            dma((NY,)),
+            dma((NX, 3, 2)),
+            dma((NY + 1, 3)),
             dma((NZ // 2,)),
             dma((3, 3)),
             dma((2, 3, 2)),
             dma((2, 3)),
-            dma((2,)),
-            dma((1,)),
-            dma((NX,)),
-            dma((4, 2)),
+            dma((2, 3)),
+            dma((3,)),
+            dma((NX, 3)),
+            dma((NY, 3)),
             dma((NX,)),
             dma((2,)),
         ],

time: 101 us -> 108 us (1.069)
  the two profiles are of different devices: /device:TPU:105 before, /device:TPU:1 now
where the time goes in v2:
time: 108 us; the launch traced here: 107 us
  Pallas kernels  105 us (97%)
  local copies, waits for them, and re-layouts  2.03 us (2%)
    pallas_call x1, Pallas kernels, local(): pl.pallas_call(kernel, out_shape=jax.ShapeDtypeStruct((2, columns, 8 * co...  105 us

profile of v2, /device:TPU:1, one launch (start us, length us, event | category | flops | bytes accessed | tf_op | source)
XLA Modules:
  0.0 106.8 jit_solution(13727757012309541356)
XLA Ops:
  0.0 0.0 copy-start
  0.0 0.0 copy-start.1
  0.0 0.0 copy-start.2
  0.0 0.0 copy-start.3
  0.0 1.1 %copy.6 = bf16[72,2,3,512]{3,0,1,2:T(8,128)(2,1)S(1)} copy(bf16[72,2,3,512]{3,0,2,1:T(8,128)(2,1)} %bitcast.11) | data formatting | bytes 884736 | tf_op jit(solution)/shard_map/reshape | solution.py:403
  1.1 0.0 copy-done
  1.1 0.0 copy-done.1
  1.1 0.0 copy-done.2
  1.1 0.0 copy-done.3
  1.2 104.7 %shard_map.55 = f32[2,72,576]{2,1,0:T(8,128)S(1)} custom-call(bf16[3,144,512]{2,1,0:T(8,128)(2,1)S(1)} %bitcast.7, f32[1,512]{1,0:T(1,128)S(1)} %bitcast.9, s32[1,512]{1,0:T(1,128)S(1)} %bitcast.10, s32[8,8]{1,0:T(8,128)S(1)} %copy-done, f32[4,4]{1,0:T(4,128)S(1)} %copy-done.3), custom_call_target="tpu_custom_call" | custom-call | tf_op jit(solution)/shard_map/pallas_call | solution.py:411
  105.9 0.9 copy.7
Async XLA Ops:
  0.0 1.1 %copy-start = (s32[8,8]{1,0:T(8,128)S(1)}, s32[8,8]{1,0:T(8,128)}, u32[]{:S(2)}) copy-start(s32[8,8]{1,0:T(8,128)} %case_ref.1) | copy-start | bytes 772
  0.0 1.1 %copy-start.1 = (f32[512]{0:T(512)S(1)}, f32[512]{0:T(512)}, u32[]{:S(2)}) copy-start(f32[512]{0:T(512)} %param.6) | copy-start | bytes 6148
  0.0 1.1 %copy-start.2 = (s32[512]{0:T(512)S(1)}, s32[512]{0:T(512)}, u32[]{:S(2)}) copy-start(s32[512]{0:T(512)} %param.7) | copy-start | bytes 6148
  0.0 1.1 %copy-start.3 = (f32[4,4]{1,0:T(4,128)S(1)}, f32[4,4]{1,0:T(4,128)}, u32[]{:S(2)}) copy-start(f32[4,4]{1,0:T(4,128)} %gain_ref.1) | copy-start | bytes 196

commit v3 on v2

--- a/solution.py
+++ b/solution.py
@@ -19,7 +19,7 @@
 
 def kernel(
     v_ref, weight_ref, group_ref, case_ref, gain_ref, out_ref,
-    rbuf, cbuf, scale, coef, acc, own, tbuf, ybuf, piece, obuf,
+    rbuf, cbuf, scale, acc, own, tbuf, ybuf, piece, obuf,
     rsem, csem, ysem, osem, own_sem, near_sem, far_sem, cown_sem, cfwd_sem,
     part_sem, ysend_sem, osend_sem, local_sem,
 ):
@@ -39,11 +39,12 @@
     def chip_x(offset):
         return lax.rem(x + offset + NX, NX)
 
-    def final_owner(k):
-        return (tile_row, NX * zl + k, y)
-
-    is_final_self = jnp.logical_and(core == zl, col // NX == zl)
-    final_self = lax.rem(col, NX)
+    def chip_y(offset):
+        return lax.rem(y + offset + NY, NY)
+
+    is_final_self = jnp.logical_and(
+        jnp.logical_and(core == zl, col == NX * zl + lax.rem(y, NX)), y // NX == lax.rem(y, 2)
+    )
 
     barrier = pltpu.get_barrier_semaphore()
 
@@ -55,15 +56,15 @@
             greet(device(x, chip_z(dirn), k, y))
         greet(device(chip_x(dirn), z, core, y))
     greet(device(x, z, 1 - core, y))
-    for step in (1, NY - 1):
-        greet((row, col, lax.rem(y + step, NY)))
+    for offset in (1, -1, 2, -2):
+        greet((row, col, chip_y(offset)))
     for h in range(NZ // 2):
         source_row = NX * (col // NX) + x
         source_col = 2 * h + zl
         @pl.when(jnp.logical_not(jnp.logical_and(is_final_self, h == zh)))
         def _():
-            greet((source_row, source_col, y))
-    pl.semaphore_wait(barrier, 13 - jnp.where(is_final_self, 1, 0))
+            greet((source_row, source_col, NX * lax.rem(y, 2) + lax.rem(col, NX)))
+    pl.semaphore_wait(barrier, 15 - jnp.where(is_final_self, 1, 0))
 
     def remote(src, dst, send, recv, target):
         return pltpu.make_async_remote_copy(
@@ -98,8 +99,9 @@
     for c in range(3):
         own_copy(0, c).start()
         own_copy(1, c).start()
-        cown_copy(0, c).start()
-        cown_copy(1, c).start()
+        if c == 0:
+            cown_copy(0, c).start()
+            cown_copy(1, c).start()
         part_copy(0, c).start()
         @pl.when(odd == 1)
         def _():
@@ -109,24 +111,18 @@
     def _():
         local_r.start()
 
-    lanes = lax.broadcasted_iota(jnp.int32, (1, coef.shape[1]), 1)
-    imag = lanes < 0
-    for m in range(8):
-        lo = m * 2 * rows + rows
-        imag = jnp.logical_or(imag, jnp.logical_and(lanes >= lo, lanes < lo + rows))
-    sign = jnp.zeros(lanes.shape, jnp.float32)
+    lanes = lax.broadcasted_iota(jnp.int32, (1, acc.shape[2]), 1)
+    imag = jnp.logical_or(
+        jnp.logical_and(lanes >= rows, lanes < 2 * rows),
+        jnp.logical_and(lanes >= 3 * rows, lanes < 4 * rows),
+    )
     for k in range(NX):
-        tile_col = NX * zl + k
-        case = case_ref[tile_row, tile_col]
+        case = case_ref[tile_row, NX * zl + k]
         groups = group_ref[...]
         gain = jnp.zeros(groups.shape, jnp.float32)
         for g in range(gain_ref.shape[0]):
             gain = jnp.where(groups == g, gain_ref[g, case], gain)
         scale[pl.ds(k, 1), :] = weight_ref[...] * gain
-        tile_sign = jnp.where(tile_row <= tile_col, 1.0, -1.0).astype(jnp.float32)
-        sign = jnp.where(lanes >= pair_rows * k, tile_sign, sign)
-    coef[pl.ds(0, 1), :] = jnp.where(imag, -sign, 1.0)
-    coef[pl.ds(1, 1), :] = jnp.where(imag, 1.0, sign)
 
     def slot(offset):
         return chip_z(offset) // 2
@@ -184,6 +180,10 @@
     def c_step(c):
         c_arrival(chip_x(back), c, core).wait_recv()
         cfwd_copy(c).start()
+        @pl.when(c < 2)
+        def _():
+            cown_copy(0, c + 1).start()
+            cown_copy(1, c + 1).start()
         c_arrival(chip_x(-back), c, core).wait_recv()
         part_copy(1, c).start()
         part_copy(3, c).start()
@@ -202,96 +202,74 @@
         odd_offset = (2 * lax.rem(pair, 2) - 1) * (1 + 2 * (pair // 2))
         return slot(jnp.where(odd == 1, odd_offset, even_offset))
 
-    third = own.shape[3]
-
-    def role(pair, k):
-        delta = lax.rem(y - (2 * pair_slot(pair) + k) + NY, NY)
-        longest = NY // 2 - k
-        down = delta <= longest
-        stage = jnp.where(down, longest - delta, delta - (longest + 1))
-        return delta, down, stage
-
-    def ysend(pair, k, q):
-        delta, down, _ = role(pair, k)
-        unit = 2 * pair + k
-        there = jnp.where(delta == NY - 1, NY, unit)
-        to = lax.rem(y + jnp.where(down, NY - 1, 1), NY)
-        return remote(
-            tbuf.at[unit, q], ybuf.at[there, q], ysend_sem.at[unit, q], ysem.at[there, q],
-            (row, col, to),
-        )
-
-    def y_arrival(unit, q):
-        return remote(
-            ybuf.at[unit, q], ybuf.at[unit, q], own_sem.at[0, 0], ysem.at[unit, q],
-            (row, col, lax.rem(y + 1, NY)),
-        )
+    def ysend(pair, i):
+        flip = lax.rem(y, 2)
+        hop = (-1, 1, -1, 1, -2 + 4 * flip, -2, 2)[i]
+        there = (0, 1, 4, 6, 5, 2, 3)[i]
+        return remote(
+            tbuf.at[pair, i], ybuf.at[pair, there], ysend_sem.at[pair, i],
+            ysem.at[pair, there], (row, col, chip_y(hop)),
+        )
+
+    def y_arrival(pair, i):
+        return remote(
+            ybuf.at[pair, i], ybuf.at[pair, i], own_sem.at[0, 0], ysem.at[pair, i],
+            (row, col, chip_y(1)),
+        )
+
+    def y_value(pair, i):
+        y_arrival(pair, i).wait_recv()
+        return ybuf[pair, i].astype(jnp.float32)
 
     def finish(pair):
-        for k in range(2):
-            base = k * 2 * rows
-            top = jnp.concatenate([acc[j, base:base + rows, :] for j in range(NX)], axis=1)
-            low = jnp.concatenate([acc[j, base + rows:base + 2 * rows, :] for j in range(NX)], axis=1)
-            width = low.shape[1]
-            swapped = jnp.where(
-                imag, pltpu.roll(low, rows, 1), pltpu.roll(low, width - rows, 1)
-            )
-            total = coef[pl.ds(0, 1), :] * top + coef[pl.ds(1, 1), :] * swapped
-            delta, _, stage = role(pair, k)
-            unit = 2 * pair + k
-            is_head = jnp.logical_and(delta > 0, stage == 0)
-            @pl.when(is_head)
+        width = 4 * rows
+        for j in range(NX):
+            sign = jnp.where(tile_row <= NX * zl + j, 1.0, -1.0).astype(jnp.float32)
+            for k in range(2):
+                base = k * 2 * rows
+                top = acc[j, base:base + rows, :]
+                low = acc[j, base + rows:base + 2 * rows, :]
+                swapped = jnp.where(
+                    imag, pltpu.roll(low, rows, 1), pltpu.roll(low, acc.shape[2] - rows, 1)
+                )
+                total = jnp.where(imag, swapped - sign * top, top + sign * swapped)
+                own[pair, NX * k + j] = total[:, :width]
+        for i, delta in enumerate((1, -1, 3, -3, 4)):
+            tbuf[pair, i] = own[pair, chip_y(-delta)].astype(jnp.bfloat16)
+            ysend(pair, i).start()
+
+    def relay(pair):
+        for side in range(2):
+            total = own[pair, chip_y(-2 + 4 * side)] + y_value(pair, 4 + 2 * side)
+            @pl.when(lax.rem(y, 2) == side)
             def _():
-                for q in range(3):
-                    tbuf[unit, q] = total[:, q * third:(q + 1) * third].astype(jnp.bfloat16)
-                    ysend(pair, k, q).start()
-            @pl.when(jnp.logical_not(is_head))
+                tbuf[pair, 5 + side] = (total + y_value(pair, 5)).astype(jnp.bfloat16)
+            @pl.when(lax.rem(y, 2) != side)
             def _():
-                for q in range(3):
-                    own[unit, q] = total[:, q * third:(q + 1) * third]
-
-    def relay(pair, when):
-        for k in range(2):
-            delta, _, stage = role(pair, k)
-            unit = 2 * pair + k
-            @pl.when(jnp.logical_and(delta > 0, stage == when))
-            def _():
-                for q in range(3):
-                    y_arrival(unit, q).wait_recv()
-                    sums = own[unit, q] + ybuf[unit, q].astype(jnp.float32)
-                    tbuf[unit, q] = sums.astype(jnp.bfloat16)
-                    ysend(pair, k, q).start()
-
-    def osend(k):
-        return remote(
-            piece.at[k], obuf.at[zh], osend_sem.at[k], osem.at[zh], final_owner(k)
-        )
-
-    def is_self(k):
-        return jnp.logical_and(is_final_self, final_self == k)
+                tbuf[pair, 5 + side] = total.astype(jnp.bfloat16)
+            ysend(pair, 5 + side).start()
+
+    def osend(pair):
+        p = 2 * pair_slot(pair) + y // NX
+        target = (tile_row, NX * zl + lax.rem(y, NX), p)
+        return remote(
+            piece.at[pair], obuf.at[zh], osend_sem.at[pair], osem.at[zh], target
+        )
+
+    def is_self(pair):
+        return jnp.logical_and(is_final_self, pair_slot(pair) == y // 2)
 
     def reduce_unit(pair):
-        unit = 2 * pair + lax.rem(y, 2)
-        parts = []
-        for q in range(3):
-            y_arrival(unit, q).wait_recv()
-            y_arrival(NY, q).wait_recv()
-            parts.append(
-                own[unit, q] + ybuf[unit, q].astype(jnp.float32) + ybuf[NY, q].astype(jnp.float32)
-            )
-        total = jnp.concatenate(parts, axis=1)
-        for k in range(NX):
-            part = total[:, k * pair_rows:(k + 1) * pair_rows]
-            piece[k] = part
-            @pl.when(is_self(k))
-            def _():
-                obuf[zh] = part
-            @pl.when(jnp.logical_not(is_self(k)))
-            def _():
-                osend(k).start()
-
-    def holds(pair):
-        return pair_slot(pair) == y // 2
+        total = own[pair, y]
+        for i in range(4):
+            total = total + y_value(pair, i)
+        @pl.when(is_self(pair))
+        def _():
+            obuf[zh] = total
+        @pl.when(jnp.logical_not(is_self(pair)))
+        def _():
+            piece[pair] = total
+            osend(pair).start()
 
     def step_body(n, carry):
         pair, c = n // 3, lax.rem(n, 3)
@@ -323,34 +301,27 @@
             )
             @pl.when(c == 0)
             def _():
-                acc[k] = product
+                acc[k, :, :pair_rows] = product
             @pl.when(c > 0)
             def _():
-                acc[k] = acc[k] + product
+                acc[k, :, :pair_rows] = acc[k, :, :pair_rows] + product
         @pl.when(c == 2)
         def _():
             finish(pair)
-        @pl.when(pair > 0)
-        def _():
-            relay(pair - 1, c + 1)
-        @pl.when(jnp.logical_and(jnp.logical_and(pair > 1, c == 0), holds(pair - 2)))
+        @pl.when(jnp.logical_and(pair > 0, c == 1))
+        def _():
+            relay(pair - 1)
+        @pl.when(jnp.logical_and(pair > 1, c == 0))
         def _():
             reduce_unit(pair - 2)
         return carry
 
+    for k in range(NX):
+        acc[k, :, pair_rows:] = jnp.zeros((pair_rows, acc.shape[2] - pair_rows), jnp.float32)
     lax.fori_loop(0, 12, step_body, 0)
-
-    def tail_body(n, carry):
-        relay(3, n + 1)
-        @pl.when(jnp.logical_and(n == 0, holds(2)))
-        def _():
-            reduce_unit(2)
-        return carry
-
-    lax.fori_loop(0, 3, tail_body, 0)
-    @pl.when(holds(3))
-    def _():
-        reduce_unit(3)
+    reduce_unit(2)
+    relay(3)
+    reduce_unit(3)
 
     for h in range(NZ // 2):
         @pl.when(jnp.logical_not(jnp.logical_and(is_final_self, h == zh)))
@@ -386,15 +357,11 @@
         for offset in range(NX):
             part_copy(offset, c).wait_send()
     for pair in range(4):
-        for k in range(2):
-            @pl.when(role(pair, k)[0] > 0)
-            def _():
-                for q in range(3):
-                    ysend(pair, k, q).wait_send()
-    for k in range(NX):
-        @pl.when(jnp.logical_not(is_self(k)))
-        def _():
-            osend(k).wait_send()
+        for i in range(7):
+            ysend(pair, i).wait_send()
+        @pl.when(jnp.logical_not(is_self(pair)))
+        def _():
+            osend(pair).wait_send()
 
 
 def local(velocity, panel_weight, panel_group, tile_map, group_gain):
@@ -404,7 +371,6 @@
     blocks = blocks.reshape(half, 2 * columns, slab)
     block = (half, 2, 2 * columns, slab)
     pair_rows = 4 * columns
-    third = NX * pair_rows // 3
     vmem = pl.BlockSpec(memory_space=pltpu.VMEM)
     smem = pl.BlockSpec(memory_space=pltpu.SMEM)
     dma = pltpu.SemaphoreType.DMA
@@ -417,16 +383,15 @@
             pltpu.VMEM((NZ // 2,) + block, jnp.bfloat16),
             pltpu.VMEM((NX,) + block, jnp.bfloat16),
             pltpu.VMEM((NX, slab), jnp.float32),
-            pltpu.VMEM((2, NX * pair_rows), jnp.float32),
-            pltpu.VMEM((NX, pair_rows, pair_rows), jnp.float32),
-            pltpu.VMEM((NY, 3, columns, third), jnp.float32),
-            pltpu.VMEM((NY, 3, columns, third), jnp.bfloat16),
-            pltpu.VMEM((NY + 1, 3, columns, third), jnp.bfloat16),
+            pltpu.VMEM((NX, pair_rows, pl.cdiv(pair_rows, 128) * 128), jnp.float32),
+            pltpu.VMEM((4, NY, columns, pair_rows), jnp.float32),
+            pltpu.VMEM((4, 7, columns, pair_rows), jnp.bfloat16),
+            pltpu.VMEM((4, 7, columns, pair_rows), jnp.bfloat16),
             pltpu.VMEM((NX, columns, pair_rows), jnp.float32),
             pltpu.VMEM((NZ // 2, columns, pair_rows), jnp.float32),
             dma((NZ // 2, 3, 2)),
             dma((NX, 3, 2)),
-            dma((NY + 1, 3)),
+            dma((4, 7)),
             dma((NZ // 2,)),
             dma((3, 3)),
             dma((2, 3, 2)),
@@ -434,7 +399,7 @@
             dma((2, 3)),
             dma((3,)),
             dma((NX, 3)),
-            dma((NY, 3)),
+            dma((4, 7)),
             dma((NX,)),
             dma((2,)),
         ],

time: 108 us -> 99.8 us (0.924)
  the two profiles are of different devices: /device:TPU:1 before, /device:TPU:384 now
where the time goes in v3:
time: 99.8 us; the launch traced here: 99.7 us
  Pallas kernels  97.6 us (98%)
  local copies, waits for them, and re-layouts  2.03 us (2%)
    pallas_call x1, Pallas kernels, local(): pl.pallas_call(kernel, out_shape=jax.ShapeDtypeStruct((2, columns, 8 * co...  97.6 us

profile of v3, /device:TPU:384, one launch (start us, length us, event | category | flops | bytes accessed | tf_op | source)
XLA Modules:
  0.0 99.7 jit_solution(15246124608019126495)
XLA Ops:
  0.0 0.0 copy-start
  0.0 0.0 copy-start.1
  0.0 0.0 copy-start.2
  0.0 0.0 copy-start.3
  0.0 1.1 %copy.6 = bf16[72,2,3,512]{3,0,1,2:T(8,128)(2,1)S(1)} copy(bf16[72,2,3,512]{3,0,2,1:T(8,128)(2,1)} %bitcast.11) | data formatting | bytes 884736 | tf_op jit(solution)/shard_map/reshape | solution.py:370
  1.1 0.0 copy-done
  1.1 0.0 copy-done.1
  1.1 0.0 copy-done.2
  1.1 0.0 copy-done.3
  1.2 97.6 %shard_map.55 = f32[2,72,576]{2,1,0:T(8,128)S(1)} custom-call(bf16[3,144,512]{2,1,0:T(8,128)(2,1)S(1)} %bitcast.7, f32[1,512]{1,0:T(1,128)S(1)} %bitcast.9, s32[1,512]{1,0:T(1,128)S(1)} %bitcast.10, s32[8,8]{1,0:T(8,128)S(1)} %copy-done, f32[4,4]{1,0:T(4,128)S(1)} %copy-done.3), custom_call_target="tpu_custom_call" | custom-call | tf_op jit(solution)/shard_map/pallas_call | solution.py:377
  98.8 0.9 copy.7
Async XLA Ops:
  0.0 1.1 %copy-start = (s32[8,8]{1,0:T(8,128)S(1)}, s32[8,8]{1,0:T(8,128)}, u32[]{:S(2)}) copy-start(s32[8,8]{1,0:T(8,128)} %case_ref.1) | copy-start | bytes 772
  0.0 1.1 %copy-start.1 = (f32[512]{0:T(512)S(1)}, f32[512]{0:T(512)}, u32[]{:S(2)}) copy-start(f32[512]{0:T(512)} %param.6) | copy-start | bytes 6148
  0.0 1.1 %copy-start.2 = (s32[512]{0:T(512)S(1)}, s32[512]{0:T(512)}, u32[]{:S(2)}) copy-start(s32[512]{0:T(512)} %param.7) | copy-start | bytes 6148
  0.0 1.1 %copy-start.3 = (f32[4,4]{1,0:T(4,128)S(1)}, f32[4,4]{1,0:T(4,128)}, u32[]{:S(2)}) copy-start(f32[4,4]{1,0:T(4,128)} %gain_ref.1) | copy-start | bytes 196

commit v4 on v3

--- a/solution.py
+++ b/solution.py
@@ -42,9 +42,11 @@
     def chip_y(offset):
         return lax.rem(y + offset + NY, NY)
 
-    is_final_self = jnp.logical_and(
-        jnp.logical_and(core == zl, col == NX * zl + lax.rem(y, NX)), y // NX == lax.rem(y, 2)
-    )
+    mine = lax.rem(y, NX)
+    is_final_self = jnp.logical_and(core == zl, col == NX * zl + mine)
+
+    def is_local(h, g):
+        return jnp.logical_and(is_final_self, jnp.logical_and(h == zh, g == y // NX))
 
     barrier = pltpu.get_barrier_semaphore()
 
@@ -59,12 +61,12 @@
     for offset in (1, -1, 2, -2):
         greet((row, col, chip_y(offset)))
     for h in range(NZ // 2):
-        source_row = NX * (col // NX) + x
-        source_col = 2 * h + zl
-        @pl.when(jnp.logical_not(jnp.logical_and(is_final_self, h == zh)))
-        def _():
-            greet((source_row, source_col, NX * lax.rem(y, 2) + lax.rem(col, NX)))
-    pl.semaphore_wait(barrier, 15 - jnp.where(is_final_self, 1, 0))
+        for g in range(2):
+            source = (NX * (col // NX) + x, 2 * h + zl, NX * g + lax.rem(col, NX))
+            @pl.when(jnp.logical_not(is_local(h, g)))
+            def _():
+                greet(source)
+    pl.semaphore_wait(barrier, 19 - jnp.where(is_final_self, 1, 0))
 
     def remote(src, dst, send, recv, target):
         return pltpu.make_async_remote_copy(
@@ -203,12 +205,10 @@
         return slot(jnp.where(odd == 1, odd_offset, even_offset))
 
     def ysend(pair, i):
-        flip = lax.rem(y, 2)
-        hop = (-1, 1, -1, 1, -2 + 4 * flip, -2, 2)[i]
-        there = (0, 1, 4, 6, 5, 2, 3)[i]
-        return remote(
-            tbuf.at[pair, i], ybuf.at[pair, there], ysend_sem.at[pair, i],
-            ysem.at[pair, there], (row, col, chip_y(hop)),
+        hop = (1, -1, 4 * lax.rem(y, 2) - 2)[i]
+        return remote(
+            tbuf.at[pair, lax.rem(chip_y(hop), NX)], ybuf.at[pair, i], ysend_sem.at[pair, i],
+            ysem.at[pair, i], (row, col, chip_y(hop)),
         )
 
     def y_arrival(pair, i):
@@ -217,14 +217,10 @@
             (row, col, chip_y(1)),
         )
 
-    def y_value(pair, i):
-        y_arrival(pair, i).wait_recv()
-        return ybuf[pair, i].astype(jnp.float32)
-
     def finish(pair):
-        width = 4 * rows
         for j in range(NX):
             sign = jnp.where(tile_row <= NX * zl + j, 1.0, -1.0).astype(jnp.float32)
+            halves = []
             for k in range(2):
                 base = k * 2 * rows
                 top = acc[j, base:base + rows, :]
@@ -232,44 +228,41 @@
                 swapped = jnp.where(
                     imag, pltpu.roll(low, rows, 1), pltpu.roll(low, acc.shape[2] - rows, 1)
                 )
-                total = jnp.where(imag, swapped - sign * top, top + sign * swapped)
-                own[pair, NX * k + j] = total[:, :width]
-        for i, delta in enumerate((1, -1, 3, -3, 4)):
-            tbuf[pair, i] = own[pair, chip_y(-delta)].astype(jnp.bfloat16)
+                halves.append(jnp.where(imag, swapped - sign * top, top + sign * swapped))
+            total = jnp.concatenate(halves, axis=0)[:, :pair_rows]
+            @pl.when(mine == j)
+            def _():
+                own[pair] = total
+            @pl.when(mine != j)
+            def _():
+                tbuf[pair, j] = total.astype(jnp.bfloat16)
+        for i in range(3):
             ysend(pair, i).start()
 
+    def osend(pair, k):
+        target = (tile_row, NX * zl + mine, 2 * pair_slot(pair) + k)
+        there = y // NX
+        return remote(
+            piece.at[pair, k], obuf.at[zh, there], osend_sem.at[pair, k], osem.at[zh, there], target
+        )
+
+    def is_self(pair, k):
+        return jnp.logical_and(is_final_self, 2 * pair_slot(pair) + k == y)
+
     def relay(pair):
-        for side in range(2):
-            total = own[pair, chip_y(-2 + 4 * side)] + y_value(pair, 4 + 2 * side)
-            @pl.when(lax.rem(y, 2) == side)
-            def _():
-                tbuf[pair, 5 + side] = (total + y_value(pair, 5)).astype(jnp.bfloat16)
-            @pl.when(lax.rem(y, 2) != side)
-            def _():
-                tbuf[pair, 5 + side] = total.astype(jnp.bfloat16)
-            ysend(pair, 5 + side).start()
-
-    def osend(pair):
-        p = 2 * pair_slot(pair) + y // NX
-        target = (tile_row, NX * zl + lax.rem(y, NX), p)
-        return remote(
-            piece.at[pair], obuf.at[zh], osend_sem.at[pair], osem.at[zh], target
-        )
-
-    def is_self(pair):
-        return jnp.logical_and(is_final_self, pair_slot(pair) == y // 2)
-
-    def reduce_unit(pair):
-        total = own[pair, y]
-        for i in range(4):
-            total = total + y_value(pair, i)
-        @pl.when(is_self(pair))
-        def _():
-            obuf[zh] = total
-        @pl.when(jnp.logical_not(is_self(pair)))
-        def _():
-            piece[pair] = total
-            osend(pair).start()
+        total = own[pair]
+        for i in range(3):
+            y_arrival(pair, i).wait_recv()
+            total = total + ybuf[pair, i].astype(jnp.float32)
+        for k in range(2):
+            half = total[k * rows:(k + 1) * rows, :].astype(jnp.bfloat16)
+            @pl.when(is_self(pair, k))
+            def _():
+                obuf[zh, y // NX] = half
+            @pl.when(jnp.logical_not(is_self(pair, k)))
+            def _():
+                piece[pair, k] = half
+                osend(pair, k).start()
 
     def step_body(n, carry):
         pair, c = n // 3, lax.rem(n, 3)
@@ -308,29 +301,26 @@
         @pl.when(c == 2)
         def _():
             finish(pair)
-        @pl.when(jnp.logical_and(pair > 0, c == 1))
+        @pl.when(jnp.logical_and(pair > 0, c == 2))
         def _():
             relay(pair - 1)
-        @pl.when(jnp.logical_and(pair > 1, c == 0))
-        def _():
-            reduce_unit(pair - 2)
         return carry
 
     for k in range(NX):
         acc[k, :, pair_rows:] = jnp.zeros((pair_rows, acc.shape[2] - pair_rows), jnp.float32)
     lax.fori_loop(0, 12, step_body, 0)
-    reduce_unit(2)
     relay(3)
-    reduce_unit(3)
-
+
+    got = []
     for h in range(NZ // 2):
-        @pl.when(jnp.logical_not(jnp.logical_and(is_final_self, h == zh)))
-        def _():
-            remote(
-                obuf.at[h], obuf.at[h], own_sem.at[0, 0], osem.at[h],
-                device(x, z, 1 - core, y),
-            ).wait_recv()
-    got = [obuf[h] for h in range(NZ // 2)]
+        for g in range(2):
+            @pl.when(jnp.logical_not(is_local(h, g)))
+            def _():
+                remote(
+                    obuf.at[h, g], obuf.at[h, g], own_sem.at[0, 0], osem.at[h, g],
+                    device(x, z, 1 - core, y),
+                ).wait_recv()
+        got.append(obuf[h, 0].astype(jnp.float32) + obuf[h, 1].astype(jnp.float32))
     for ri in range(2):
         out_ref[ri] = jnp.concatenate(
             [got[h][:, (2 * k + ri) * rows:(2 * k + ri + 1) * rows]
@@ -357,11 +347,12 @@
         for offset in range(NX):
             part_copy(offset, c).wait_send()
     for pair in range(4):
-        for i in range(7):
+        for i in range(3):
             ysend(pair, i).wait_send()
-        @pl.when(jnp.logical_not(is_self(pair)))
-        def _():
-            osend(pair).wait_send()
+        for k in range(2):
+            @pl.when(jnp.logical_not(is_self(pair, k)))
+            def _():
+                osend(pair, k).wait_send()
 
 
 def local(velocity, panel_weight, panel_group, tile_map, group_gain):
@@ -384,23 +375,23 @@
             pltpu.VMEM((NX,) + block, jnp.bfloat16),
             pltpu.VMEM((NX, slab), jnp.float32),
             pltpu.VMEM((NX, pair_rows, pl.cdiv(pair_rows, 128) * 128), jnp.float32),
-            pltpu.VMEM((4, NY, columns, pair_rows), jnp.float32),
-            pltpu.VMEM((4, 7, columns, pair_rows), jnp.bfloat16),
-            pltpu.VMEM((4, 7, columns, pair_rows), jnp.bfloat16),
-            pltpu.VMEM((NX, columns, pair_rows), jnp.float32),
-            pltpu.VMEM((NZ // 2, columns, pair_rows), jnp.float32),
+            pltpu.VMEM((4, 2 * columns, pair_rows), jnp.float32),
+            pltpu.VMEM((4, NX, 2 * columns, pair_rows), jnp.bfloat16),
+            pltpu.VMEM((4, 3, 2 * columns, pair_rows), jnp.bfloat16),
+            pltpu.VMEM((4, 2, columns, pair_rows), jnp.bfloat16),
+            pltpu.VMEM((NZ // 2, 2, columns, pair_rows), jnp.bfloat16),
             dma((NZ // 2, 3, 2)),
             dma((NX, 3, 2)),
-            dma((4, 7)),
-            dma((NZ // 2,)),
+            dma((4, 3)),
+            dma((NZ // 2, 2)),
             dma((3, 3)),
             dma((2, 3, 2)),
             dma((2, 3)),
             dma((2, 3)),
             dma((3,)),
             dma((NX, 3)),
-            dma((4, 7)),
-            dma((NX,)),
+            dma((4, 3)),
+            dma((4, 2)),
             dma((2,)),
         ],
         compiler_params=pltpu.CompilerParams(

time: 99.8 us -> 88.5 us (0.89)
  the two profiles are of different devices: /device:TPU:384 before, /device:TPU:1 now
where the time goes in v4:
time: 88.5 us; the launch traced here: 88.4 us
  Pallas kernels  86.3 us (98%)
  local copies, waits for them, and re-layouts  2.03 us (2%)
    pallas_call x1, Pallas kernels, local(): pl.pallas_call(kernel, out_shape=jax.ShapeDtypeStruct((2, columns, 8 * co...  86.3 us

profile of v4, /device:TPU:1, one launch (start us, length us, event | category | flops | bytes accessed | tf_op | source)
XLA Modules:
  0.0 88.4 jit_solution(4130302936056232864)
XLA Ops:
  0.0 0.0 copy-start
  0.0 0.0 copy-start.1
  0.0 0.0 copy-start.2
  0.0 0.0 copy-start.3
  0.0 1.1 %copy.6 = bf16[72,2,3,512]{3,0,1,2:T(8,128)(2,1)S(1)} copy(bf16[72,2,3,512]{3,0,2,1:T(8,128)(2,1)} %bitcast.11) | data formatting | bytes 884736 | tf_op jit(solution)/shard_map/reshape | solution.py:361
  1.1 0.0 copy-done
  1.1 0.0 copy-done.1
  1.1 0.0 copy-done.2
  1.1 0.0 copy-done.3
  1.2 86.3 %shard_map.55 = f32[2,72,576]{2,1,0:T(8,128)S(1)} custom-call(bf16[3,144,512]{2,1,0:T(8,128)(2,1)S(1)} %bitcast.7, f32[1,512]{1,0:T(1,128)S(1)} %bitcast.9, s32[1,512]{1,0:T(1,128)S(1)} %bitcast.10, s32[8,8]{1,0:T(8,128)S(1)} %copy-done, f32[4,4]{1,0:T(4,128)S(1)} %copy-done.3), custom_call_target="tpu_custom_call" | custom-call | tf_op jit(solution)/shard_map/pallas_call | solution.py:368
  87.5 0.9 %copy.7 = f32[72,2,576]{2,1,0:T(2,128)} copy(f32[72,2,576]{2,0,1:T(8,128)S(1)} %bitcast.8) | data formatting | bytes 663552 | tf_op jit(solution)/shard_map/transpose | solution.py:401
Async XLA Ops:
  0.0 1.1 %copy-start = (s32[8,8]{1,0:T(8,128)S(1)}, s32[8,8]{1,0:T(8,128)}, u32[]{:S(2)}) copy-start(s32[8,8]{1,0:T(8,128)} %case_ref.1) | copy-start | bytes 772
  0.0 1.1 %copy-start.1 = (f32[512]{0:T(512)S(1)}, f32[512]{0:T(512)}, u32[]{:S(2)}) copy-start(f32[512]{0:T(512)} %param.6) | copy-start | bytes 6148
  0.0 1.1 %copy-start.2 = (s32[512]{0:T(512)S(1)}, s32[512]{0:T(512)}, u32[]{:S(2)}) copy-start(s32[512]{0:T(512)} %param.7) | copy-start | bytes 6148
  0.0 1.1 %copy-start.3 = (f32[4,4]{1,0:T(4,128)S(1)}, f32[4,4]{1,0:T(4,128)}, u32[]{:S(2)}) copy-start(f32[4,4]{1,0:T(4,128)} %gain_ref.1) | copy-start | bytes 196

commit v5 on v4

--- a/solution.py
+++ b/solution.py
@@ -217,6 +217,25 @@
             (row, col, chip_y(1)),
         )
 
+    lane_cut = ybuf.shape[3]
+    left_over = pair_rows - lane_cut
+    group = rows // 3
+
+    def pack(halves):
+        rest = [
+            half[g * group:(g + 1) * group, lane_cut:pair_rows] for half in halves for g in range(3)
+        ]
+        rest.append(jnp.zeros((group, lane_cut - 6 * left_over), jnp.float32))
+        return jnp.concatenate(
+            [half[:, :lane_cut] for half in halves] + [jnp.concatenate(rest, axis=1)], axis=0
+        )
+
+    def unpack(half):
+        rest = jnp.concatenate(
+            [half[rows:rows + group, g * left_over:(g + 1) * left_over] for g in range(3)], axis=0
+        )
+        return jnp.concatenate([half[:rows, :], rest], axis=1)
+
     def finish(pair):
         for j in range(NX):
             sign = jnp.where(tile_row <= NX * zl + j, 1.0, -1.0).astype(jnp.float32)
@@ -229,7 +248,7 @@
                     imag, pltpu.roll(low, rows, 1), pltpu.roll(low, acc.shape[2] - rows, 1)
                 )
                 halves.append(jnp.where(imag, swapped - sign * top, top + sign * swapped))
-            total = jnp.concatenate(halves, axis=0)[:, :pair_rows]
+            total = pack(halves)
             @pl.when(mine == j)
             def _():
                 own[pair] = total
@@ -255,7 +274,11 @@
             y_arrival(pair, i).wait_recv()
             total = total + ybuf[pair, i].astype(jnp.float32)
         for k in range(2):
-            half = total[k * rows:(k + 1) * rows, :].astype(jnp.bfloat16)
+            rest = total[2 * rows:2 * rows + group, :]
+            if k == 1:
+                rest = jnp.concatenate([rest[:, 3 * left_over:], rest[:, :3 * left_over]], axis=1)
+            half = jnp.concatenate([total[k * rows:(k + 1) * rows, :], rest], axis=0)
+            half = half.astype(jnp.bfloat16)
             @pl.when(is_self(pair, k))
             def _():
                 obuf[zh, y // NX] = half
@@ -301,14 +324,15 @@
         @pl.when(c == 2)
         def _():
             finish(pair)
-        @pl.when(jnp.logical_and(pair > 0, c == 2))
-        def _():
-            relay(pair - 1)
+        @pl.when(n >= 10)
+        def _():
+            relay(n - 10)
         return carry
 
     for k in range(NX):
         acc[k, :, pair_rows:] = jnp.zeros((pair_rows, acc.shape[2] - pair_rows), jnp.float32)
     lax.fori_loop(0, 12, step_body, 0)
+    relay(2)
     relay(3)
 
     got = []
@@ -320,7 +344,7 @@
                     obuf.at[h, g], obuf.at[h, g], own_sem.at[0, 0], osem.at[h, g],
                     device(x, z, 1 - core, y),
                 ).wait_recv()
-        got.append(obuf[h, 0].astype(jnp.float32) + obuf[h, 1].astype(jnp.float32))
+        got.append(unpack(obuf[h, 0].astype(jnp.float32) + obuf[h, 1].astype(jnp.float32)))
     for ri in range(2):
         out_ref[ri] = jnp.concatenate(
             [got[h][:, (2 * k + ri) * rows:(2 * k + ri + 1) * rows]
@@ -362,6 +386,9 @@
     blocks = blocks.reshape(half, 2 * columns, slab)
     block = (half, 2, 2 * columns, slab)
     pair_rows = 4 * columns
+    lane_cut = pair_rows // 128 * 128
+    packed = (2 * columns + columns // 3, lane_cut)
+    packed_half = (columns + columns // 3, lane_cut)
     vmem = pl.BlockSpec(memory_space=pltpu.VMEM)
     smem = pl.BlockSpec(memory_space=pltpu.SMEM)
     dma = pltpu.SemaphoreType.DMA
@@ -375,11 +402,11 @@
             pltpu.VMEM((NX,) + block, jnp.bfloat16),
             pltpu.VMEM((NX, slab), jnp.float32),
             pltpu.VMEM((NX, pair_rows, pl.cdiv(pair_rows, 128) * 128), jnp.float32),
-            pltpu.VMEM((4, 2 * columns, pair_rows), jnp.float32),
-            pltpu.VMEM((4, NX, 2 * columns, pair_rows), jnp.bfloat16),
-            pltpu.VMEM((4, 3, 2 * columns, pair_rows), jnp.bfloat16),
-            pltpu.VMEM((4, 2, columns, pair_rows), jnp.bfloat16),
-            pltpu.VMEM((NZ // 2, 2, columns, pair_rows), jnp.bfloat16),
+            pltpu.VMEM((4,) + packed, jnp.float32),
+            pltpu.VMEM((4, NX) + packed, jnp.bfloat16),
+            pltpu.VMEM((4, 3) + packed, jnp.bfloat16),
+            pltpu.VMEM((4, 2) + packed_half, jnp.bfloat16),
+            pltpu.VMEM((NZ // 2, 2) + packed_half, jnp.bfloat16),
             dma((NZ // 2, 3, 2)),
             dma((NX, 3, 2)),
             dma((4, 3)),

time: 88.5 us -> 84.2 us (0.951)
  Pallas kernels: 86.3 us -> 81.9 us
    pallas_call x1, Pallas kernels: 86.3 us -> 81.9 us  [local(): pl.pallas_call(kernel, out_shape=jax.ShapeDtypeStruct((2, columns, 8 * co...]
where the time goes in v5:
time: 84.2 us; the launch traced here: 84 us
  Pallas kernels  81.9 us (97%)
  local copies, waits for them, and re-layouts  2.03 us (2%)
    pallas_call x1, Pallas kernels, local(): pl.pallas_call(kernel, out_shape=jax.ShapeDtypeStruct((2, columns, 8 * co...  81.9 us

profile of v5, /device:TPU:1, one launch (start us, length us, event | category | flops | bytes accessed | tf_op | source)
XLA Modules:
  0.0 84.0 jit_solution(7946707731265214705)
XLA Ops:
  0.0 0.0 copy-start
  0.0 0.0 copy-start.1
  0.0 0.0 copy-start.2
  0.0 0.0 copy-start.3
  0.0 1.1 %copy.6 = bf16[72,2,3,512]{3,0,1,2:T(8,128)(2,1)S(1)} copy(bf16[72,2,3,512]{3,0,2,1:T(8,128)(2,1)} %bitcast.11) | data formatting | bytes 884736 | tf_op jit(solution)/shard_map/reshape | solution.py:385
  1.1 0.0 copy-done
  1.1 0.0 copy-done.1
  1.1 0.0 copy-done.2
  1.1 0.0 copy-done.3
  1.2 81.9 %shard_map.55 = f32[2,72,576]{2,1,0:T(8,128)S(1)} custom-call(bf16[3,144,512]{2,1,0:T(8,128)(2,1)S(1)} %bitcast.7, f32[1,512]{1,0:T(1,128)S(1)} %bitcast.9, s32[1,512]{1,0:T(1,128)S(1)} %bitcast.10, s32[8,8]{1,0:T(8,128)S(1)} %copy-done, f32[4,4]{1,0:T(4,128)S(1)} %copy-done.3), custom_call_target="tpu_custom_call" | custom-call | tf_op jit(solution)/shard_map/pallas_call | solution.py:395
  83.1 0.9 %copy.7 = f32[72,2,576]{2,1,0:T(2,128)} copy(f32[72,2,576]{2,0,1:T(8,128)S(1)} %bitcast.8) | data formatting | bytes 663552 | tf_op jit(solution)/shard_map/transpose | solution.py:428
Async XLA Ops:
  0.0 1.1 %copy-start = (s32[8,8]{1,0:T(8,128)S(1)}, s32[8,8]{1,0:T(8,128)}, u32[]{:S(2)}) copy-start(s32[8,8]{1,0:T(8,128)} %case_ref.1) | copy-start | bytes 772
  0.0 1.1 %copy-start.1 = (f32[512]{0:T(512)S(1)}, f32[512]{0:T(512)}, u32[]{:S(2)}) copy-start(f32[512]{0:T(512)} %param.6) | copy-start | bytes 6148
  0.0 1.1 %copy-start.2 = (s32[512]{0:T(512)S(1)}, s32[512]{0:T(512)}, u32[]{:S(2)}) copy-start(s32[512]{0:T(512)} %param.7) | copy-start | bytes 6148
  0.0 1.1 %copy-start.3 = (f32[4,4]{1,0:T(4,128)S(1)}, f32[4,4]{1,0:T(4,128)}, u32[]{:S(2)}) copy-start(f32[4,4]{1,0:T(4,128)} %gain_ref.1) | copy-start | bytes 196

commit v6 on v5

--- a/solution.py
+++ b/solution.py
@@ -21,7 +21,7 @@
     v_ref, weight_ref, group_ref, case_ref, gain_ref, out_ref,
     rbuf, cbuf, scale, acc, own, tbuf, ybuf, piece, obuf,
     rsem, csem, ysem, osem, own_sem, near_sem, far_sem, cown_sem, cfwd_sem,
-    part_sem, ysend_sem, osend_sem, local_sem,
+    part_sem, ysend_sem, osend_sem, local_sem, inside,
 ):
     rows = v_ref.shape[1] // 2
     pair_rows = 4 * rows
@@ -39,11 +39,11 @@
     def chip_x(offset):
         return lax.rem(x + offset + NX, NX)
 
+    mine = lax.rem(y, NX)
+    is_final_self = jnp.logical_and(core == zl, col == NX * zl + mine)
+
     def chip_y(offset):
         return lax.rem(y + offset + NY, NY)
-
-    mine = lax.rem(y, NX)
-    is_final_self = jnp.logical_and(core == zl, col == NX * zl + mine)
 
     def is_local(h, g):
         return jnp.logical_and(is_final_self, jnp.logical_and(h == zh, g == y // NX))
@@ -60,13 +60,28 @@
     greet(device(x, z, 1 - core, y))
     for offset in (1, -1, 2, -2):
         greet((row, col, chip_y(offset)))
-    for h in range(NZ // 2):
-        for g in range(2):
-            source = (NX * (col // NX) + x, 2 * h + zl, NX * g + lax.rem(col, NX))
-            @pl.when(jnp.logical_not(is_local(h, g)))
-            def _():
-                greet(source)
-    pl.semaphore_wait(barrier, 19 - jnp.where(is_final_self, 1, 0))
+    pl.semaphore_wait(barrier, 11)
+
+    def tell(n):
+        @pl.when(n == 0)
+        def _():
+            for offset in (2, -2):
+                pl.semaphore_signal(
+                    inside.at[0], inc=1, device_id=(row, col, chip_y(offset)), device_id_type=MESH
+                )
+        @pl.when(n > 0)
+        def _():
+            for dirn in (1, -1):
+                for k in range(2):
+                    pl.semaphore_signal(
+                        inside.at[n], inc=1, device_id=device(x, chip_z(dirn), k, y),
+                        device_id_type=MESH,
+                    )
+
+    def hear(n):
+        pl.semaphore_wait(inside.at[n], jnp.where(n == 0, 2, 4))
+
+    tell(0)
 
     def remote(src, dst, send, recv, target):
         return pltpu.make_async_remote_copy(
@@ -237,7 +252,8 @@
         return jnp.concatenate([half[:rows, :], rest], axis=1)
 
     def finish(pair):
-        for j in range(NX):
+        for i, offset in enumerate((1, 3, 2, 0)):
+            j = lax.rem(mine + offset, NX)
             sign = jnp.where(tile_row <= NX * zl + j, 1.0, -1.0).astype(jnp.float32)
             halves = []
             for k in range(2):
@@ -248,15 +264,11 @@
                     imag, pltpu.roll(low, rows, 1), pltpu.roll(low, acc.shape[2] - rows, 1)
                 )
                 halves.append(jnp.where(imag, swapped - sign * top, top + sign * swapped))
-            total = pack(halves)
-            @pl.when(mine == j)
-            def _():
-                own[pair] = total
-            @pl.when(mine != j)
-            def _():
-                tbuf[pair, j] = total.astype(jnp.bfloat16)
-        for i in range(3):
-            ysend(pair, i).start()
+            if offset:
+                tbuf[pair, j] = pack(halves).astype(jnp.bfloat16)
+                ysend(pair, i).start()
+            else:
+                own[pair] = pack(halves)
 
     def osend(pair, k):
         target = (tile_row, NX * zl + mine, 2 * pair_slot(pair) + k)
@@ -305,9 +317,9 @@
         def _():
             for k in range(2):
                 arrival(slot(4), c, k).wait_recv()
-        @pl.when(jnp.logical_and(odd == 1, pair == 2))
-        def _():
-            far_step(c)
+        @pl.when(jnp.logical_and(odd == 1, jnp.logical_and(n >= 5, n < 8)))
+        def _():
+            far_step(n - 5)
         left = rbuf[pair_slot(pair), c].reshape(pair_rows, v_ref.shape[2]).astype(jnp.float32)
         for k in range(NX):
             weighted = (left * scale[pl.ds(k, 1), :]).astype(jnp.bfloat16)
@@ -324,6 +336,12 @@
         @pl.when(c == 2)
         def _():
             finish(pair)
+        @pl.when(jnp.logical_and(lax.rem(n, 2) == 1, n < 11))
+        def _():
+            hear(n // 2)
+            @pl.when(n < 9)
+            def _():
+                tell(n // 2 + 1)
         @pl.when(n >= 10)
         def _():
             relay(n - 10)
@@ -420,6 +438,7 @@
             dma((4, 3)),
             dma((4, 2)),
             dma((2,)),
+            pltpu.SemaphoreType.REGULAR((5,)),
         ],
         compiler_params=pltpu.CompilerParams(
             collective_id=0, has_side_effects=True, vmem_limit_bytes=40 * 1024 * 1024

time: 84.2 us -> 83.1 us (0.987)
  the two profiles are of different devices: /device:TPU:1 before, /device:TPU:8 now
where the time goes in v6:
time: 83.1 us; the launch traced here: 83 us
  Pallas kernels  80.9 us (97%)
  local copies, waits for them, and re-layouts  2.03 us (2%)
    pallas_call x1, Pallas kernels, local(): pl.pallas_call(kernel, out_shape=jax.ShapeDtypeStruct((2, columns, 8 * co...  80.9 us

profile of v6, /device:TPU:8, one launch (start us, length us, event | category | flops | bytes accessed | tf_op | source)
XLA Modules:
  0.0 83.0 jit_solution(12576286032880364430)
XLA Ops:
  0.0 0.0 copy-start
  0.0 0.0 copy-start.1
  0.0 0.0 copy-start.2
  0.0 0.0 copy-start.3
  0.0 1.1 %copy.6 = bf16[72,2,3,512]{3,0,1,2:T(8,128)(2,1)S(1)} copy(bf16[72,2,3,512]{3,0,2,1:T(8,128)(2,1)} %bitcast.11) | data formatting | bytes 884736 | tf_op jit(solution)/shard_map/reshape | solution.py:403
  1.1 0.0 copy-done
  1.1 0.0 copy-done.1
  1.1 0.0 copy-done.2
  1.1 0.0 copy-done.3
  1.2 80.9 %shard_map.55 = f32[2,72,576]{2,1,0:T(8,128)S(1)} custom-call(bf16[3,144,512]{2,1,0:T(8,128)(2,1)S(1)} %bitcast.7, f32[1,512]{1,0:T(1,128)S(1)} %bitcast.9, s32[1,512]{1,0:T(1,128)S(1)} %bitcast.10, s32[8,8]{1,0:T(8,128)S(1)} %copy-done, f32[4,4]{1,0:T(4,128)S(1)} %copy-done.3), custom_call_target="tpu_custom_call" | custom-call | tf_op jit(solution)/shard_map/pallas_call | solution.py:413
  82.0 0.9 %copy.7 = f32[72,2,576]{2,1,0:T(2,128)} copy(f32[72,2,576]{2,0,1:T(8,128)S(1)} %bitcast.8) | data formatting | bytes 663552 | tf_op jit(solution)/shard_map/transpose | solution.py:447
Async XLA Ops:
  0.0 1.1 %copy-start = (s32[8,8]{1,0:T(8,128)S(1)}, s32[8,8]{1,0:T(8,128)}, u32[]{:S(2)}) copy-start(s32[8,8]{1,0:T(8,128)} %case_ref.1) | copy-start | bytes 772
  0.0 1.1 %copy-start.1 = (f32[512]{0:T(512)S(1)}, f32[512]{0:T(512)}, u32[]{:S(2)}) copy-start(f32[512]{0:T(512)} %param.6) | copy-start | bytes 6148
  0.0 1.1 %copy-start.2 = (s32[512]{0:T(512)S(1)}, s32[512]{0:T(512)}, u32[]{:S(2)}) copy-start(s32[512]{0:T(512)} %param.7) | copy-start | bytes 6148
  0.0 1.1 %copy-start.3 = (f32[4,4]{1,0:T(4,128)S(1)}, f32[4,4]{1,0:T(4,128)}, u32[]{:S(2)}) copy-start(f32[4,4]{1,0:T(4,128)} %gain_ref.1) | copy-start | bytes 196

commit v7 on v6

--- a/solution.py
+++ b/solution.py
@@ -114,12 +114,12 @@
     local_c = pltpu.make_async_copy(v_ref, cbuf.at[x, :, core], local_sem.at[0])
     local_r = pltpu.make_async_copy(v_ref, rbuf.at[zh, :, core], local_sem.at[1])
     for c in range(3):
-        own_copy(0, c).start()
-        own_copy(1, c).start()
         if c == 0:
             cown_copy(0, c).start()
             cown_copy(1, c).start()
         part_copy(0, c).start()
+        own_copy(0, c).start()
+        own_copy(1, c).start()
         @pl.when(odd == 1)
         def _():
             own_copy(2, c).start()

time: 83.1 us -> 83.1 us (level)
  no operation moved by 1% of the time
where the time goes in v7:
time: 83.1 us; the launch traced here: 83 us
  Pallas kernels  80.9 us (97%)
  local copies, waits for them, and re-layouts  2.03 us (2%)
    pallas_call x1, Pallas kernels, local(): pl.pallas_call(kernel, out_shape=jax.ShapeDtypeStruct((2, columns, 8 * co...  80.9 us

profile of v7, /device:TPU:8, one launch (start us, length us, event | category | flops | bytes accessed | tf_op | source)
XLA Modules:
  0.0 83.0 jit_solution(7631627825380786580)
XLA Ops:
  0.0 0.0 copy-start
  0.0 0.0 copy-start.1
  0.0 0.0 copy-start.2
  0.0 0.0 copy-start.3
  0.0 1.1 %copy.6 = bf16[72,2,3,512]{3,0,1,2:T(8,128)(2,1)S(1)} copy(bf16[72,2,3,512]{3,0,2,1:T(8,128)(2,1)} %bitcast.11) | data formatting | bytes 884736 | tf_op jit(solution)/shard_map/reshape | solution.py:403
  1.1 0.0 copy-done
  1.1 0.0 copy-done.1
  1.1 0.0 copy-done.2
  1.1 0.0 copy-done.3
  1.2 80.9 %shard_map.55 = f32[2,72,576]{2,1,0:T(8,128)S(1)} custom-call(bf16[3,144,512]{2,1,0:T(8,128)(2,1)S(1)} %bitcast.7, f32[1,512]{1,0:T(1,128)S(1)} %bitcast.9, s32[1,512]{1,0:T(1,128)S(1)} %bitcast.10, s32[8,8]{1,0:T(8,128)S(1)} %copy-done, f32[4,4]{1,0:T(4,128)S(1)} %copy-done.3), custom_call_target="tpu_custom_call" | custom-call | tf_op jit(solution)/shard_map/pallas_call | solution.py:413
  82.0 0.9 %copy.7 = f32[72,2,576]{2,1,0:T(2,128)} copy(f32[72,2,576]{2,0,1:T(8,128)S(1)} %bitcast.8) | data formatting | bytes 663552 | tf_op jit(solution)/shard_map/transpose | solution.py:447
Async XLA Ops:
  0.0 1.1 %copy-start = (s32[8,8]{1,0:T(8,128)S(1)}, s32[8,8]{1,0:T(8,128)}, u32[]{:S(2)}) copy-start(s32[8,8]{1,0:T(8,128)} %case_ref.1) | copy-start | bytes 772
  0.0 1.1 %copy-start.1 = (f32[512]{0:T(512)S(1)}, f32[512]{0:T(512)}, u32[]{:S(2)}) copy-start(f32[512]{0:T(512)} %param.6) | copy-start | bytes 6148
  0.0 1.1 %copy-start.2 = (s32[512]{0:T(512)S(1)}, s32[512]{0:T(512)}, u32[]{:S(2)}) copy-start(s32[512]{0:T(512)} %param.7) | copy-start | bytes 6148
  0.0 1.1 %copy-start.3 = (f32[4,4]{1,0:T(4,128)S(1)}, f32[4,4]{1,0:T(4,128)}, u32[]{:S(2)}) copy-start(f32[4,4]{1,0:T(4,128)} %gain_ref.1) | copy-start | bytes 196
